TPU v7x, 32 devices: a whole 2x2x4 slice. The times are simulated.
32 devices in a mesh: dp: 16 (over z, x, core), opt: 2 (over y).
Axes of the slice: x: 2, y: 2, z: 4, core: 2. Of those that a mesh axis runs over, the one named last changes fastest.
Arguments:
- params: bfloat16 [12595200], P('opt'), may hold values from -2 to 2, as said below
- moment_one: float32 [12595200], P('opt'), may hold values from -160 to 160
- moment_two: float32 [12595200], P('opt'), may hold values from 81.92 to 8192
- inputs: bfloat16 [64, 128, 1024], P(('dp', 'opt')), may hold values from -6 to 6
- cotangent: bfloat16 [64, 128, 1024], P(('dp', 'opt')), may hold values from -6 to 6
- segments: int32 [64, 128], P(('dp', 'opt')), may hold values from 0 to 3, never falling along the last dimension, each value on 1 to 64 neighbouring positions
- windows: int32 [64], P(('dp', 'opt')), may hold values from 128 to 512, as said below
Outputs:
- output: bfloat16 [64, 128, 1024], P(('dp', 'opt'))
- input_grad: bfloat16 [64, 128, 1024], P(('dp', 'opt'))
- grads: float32 [12595200], P('opt')
- new_params: float32 [12595200], P('opt')
- new_moment_one: float32 [12595200], P('opt')
- new_moment_two: float32 [12595200], P('opt')
- new_copy: bfloat16 [12595200], P('opt')
Inputs may be any that keep to these rules, and one draw needn't show every extreme that they name: `params`: the flat parameter vector in the layout of the steps; gains near 1. `windows`: every draw holds a sequence with window 512 and one with window 512 // 4.
All inputs are finite; a program needn't handle non-finite values.
Results may differ from a plain program's by a relative error of at most 0.0094.
Values may be sent and summed in bfloat16 or wider, within the bound.
No kernel may reach another device: no remote copies, remote signals or barrier semaphores. Data moves between devices by JAX's collectives and lax.ppermute only.
A program may use at most 448 MiB of HBM per device.

v0:
```python
import math
import jax
import jax.numpy as jnp
from jax import lax
from jax.sharding import PartitionSpec as P

HEADS = 16
HEAD_DIM = 64
FF = 4096
MATRIX_PARAMS = 12582912
GELU_C = math.sqrt(2.0 / math.pi)
LEARN_RATE = 0.01
WEIGHT_DECAY = 0.1


def unpack_weights(flat_values, model_width, hidden_units):
    layout = [
        (model_width, 3 * model_width),
        (model_width, model_width),
        (model_width, hidden_units),
        (hidden_units, model_width),
    ]
    layout = layout + [(model_width,)] * 7 + [(hidden_units,), (model_width,)]
    pieces = []
    position = 0
    for piece_dims in layout:
        amount = math.prod(piece_dims)
        pieces.append(flat_values[position : position + amount].reshape(piece_dims))
        position = position + amount
    return pieces


def standardize(values):
    centred = values - jnp.mean(values, axis=-1, keepdims=True)
    inverse = lax.rsqrt(jnp.mean(centred * centred, axis=-1, keepdims=True) + 1e-05)
    return (centred * inverse, inverse)


def gelu_value(values):
    return 0.5 * values * (1.0 + jnp.tanh(GELU_C * (values + 0.044715 * values * values * values)))


def gelu_slope(values):
    tangent = jnp.tanh(GELU_C * (values + 0.044715 * values * values * values))
    return 0.5 * (1.0 + tangent) + 0.5 * values * (1.0 - tangent * tangent) * GELU_C * (
        1.0 + 0.134145 * values * values
    )


def norm_back(grad_norm, normed, inverse):
    return inverse * (
        grad_norm
        - jnp.mean(grad_norm, axis=-1, keepdims=True)
        - normed * jnp.mean(grad_norm * normed, axis=-1, keepdims=True)
    )


def column_sum(values):
    return jnp.sum(values.astype(jnp.float32), axis=0)


def inner_rows(left_rows, right_rows):
    return lax.dot_general(
        left_rows, right_rows, (((0,), (0,)), ((), ())), preferred_element_type=jnp.float32
    )


def sequence_pass(weights, tokens, cotangent_rows, segment_ids, window_len):
    (
        qkv_weight,
        out_weight,
        fc_weight,
        proj_weight,
        first_gain,
        first_shift,
        query_bias,
        value_bias,
        out_bias,
        second_gain,
        second_shift,
        fc_bias,
        proj_bias,
    ) = weights
    seq_rows, model_width = tokens.shape
    score_scale = 1.0 / math.sqrt(HEAD_DIM)
    first_gain_f = first_gain.astype(jnp.float32)
    second_gain_f = second_gain.astype(jnp.float32)
    residual_in = tokens.astype(jnp.float32)
    normed_one, inverse_one = standardize(residual_in)
    hidden_one = (normed_one * first_gain_f + first_shift.astype(jnp.float32)).astype(jnp.bfloat16)
    qkv_bias = jnp.concatenate([query_bias, jnp.zeros_like(query_bias), value_bias]).astype(
        jnp.float32
    )
    projected = (
        jnp.dot(hidden_one, qkv_weight, preferred_element_type=jnp.float32) + qkv_bias
    ).astype(jnp.bfloat16)
    queries = projected[:, :model_width].reshape(seq_rows, HEADS, HEAD_DIM)
    key_heads = projected[:, model_width : 2 * model_width].reshape(seq_rows, HEADS, HEAD_DIM)
    value_heads = projected[:, 2 * model_width :].reshape(seq_rows, HEADS, HEAD_DIM)
    positions = jnp.arange(seq_rows)
    allowed = (
        (positions[None, :] <= positions[:, None])
        & (positions[:, None] - positions[None, :] < window_len)
        & (segment_ids[:, None] == segment_ids[None, :])
    )

    def masked_scores():
        raw_scores = (
            jnp.einsum("qhd,khd->hqk", queries, key_heads, preferred_element_type=jnp.float32)
            * score_scale
        )
        return jnp.where(allowed[None], raw_scores, -jnp.inf)

    scores = masked_scores()
    row_max = jnp.max(scores, axis=-1, keepdims=True)
    log_total = row_max + jnp.log(jnp.sum(jnp.exp(scores - row_max), axis=-1, keepdims=True))
    probs = jnp.exp(scores - log_total).astype(jnp.bfloat16)
    mixed = jnp.einsum("hqk,khd->qhd", probs, value_heads, preferred_element_type=jnp.float32)
    mixed = mixed.reshape(seq_rows, model_width).astype(jnp.bfloat16)
    attended = jnp.dot(mixed, out_weight, preferred_element_type=jnp.float32) + out_bias.astype(
        jnp.float32
    )
    residual_mid = residual_in + attended
    normed_two, inverse_two = standardize(residual_mid)
    hidden_two = (normed_two * second_gain_f + second_shift.astype(jnp.float32)).astype(
        jnp.bfloat16
    )
    before_act = jnp.dot(
        hidden_two, fc_weight, preferred_element_type=jnp.float32
    ) + fc_bias.astype(jnp.float32)
    activated = gelu_value(before_act).astype(jnp.bfloat16)
    result_rows = jnp.dot(
        activated, proj_weight, preferred_element_type=jnp.float32
    ) + proj_bias.astype(jnp.float32)
    output_rows = (residual_mid + result_rows).astype(jnp.bfloat16)
    grad_proj = inner_rows(activated, cotangent_rows)
    grad_proj_bias = column_sum(cotangent_rows)
    grad_act = jnp.dot(cotangent_rows, proj_weight.T, preferred_element_type=jnp.float32)
    grad_before = (grad_act * gelu_slope(before_act)).astype(jnp.bfloat16)
    grad_fc = inner_rows(hidden_two, grad_before)
    grad_fc_bias = column_sum(grad_before)
    grad_hidden_two = jnp.dot(grad_before, fc_weight.T, preferred_element_type=jnp.float32)
    grad_second_gain = jnp.sum(grad_hidden_two * normed_two, axis=0)
    grad_second_shift = jnp.sum(grad_hidden_two, axis=0)
    grad_mid = cotangent_rows.astype(jnp.float32) + norm_back(
        grad_hidden_two * second_gain_f, normed_two, inverse_two
    )
    grad_attended = grad_mid.astype(jnp.bfloat16)
    grad_out = inner_rows(mixed, grad_attended)
    grad_out_bias = column_sum(grad_attended)
    grad_mixed = jnp.dot(grad_attended, out_weight.T, preferred_element_type=jnp.float32).astype(
        jnp.bfloat16
    )
    grad_mixed = grad_mixed.reshape(seq_rows, HEADS, HEAD_DIM)
    grad_probs = jnp.einsum(
        "qhd,khd->hqk", grad_mixed, value_heads, preferred_element_type=jnp.float32
    )
    exact_probs = jnp.exp(masked_scores() - log_total)
    row_terms = jnp.sum(exact_probs * grad_probs, axis=-1, keepdims=True)
    grad_scores = (exact_probs * (grad_probs - row_terms)).astype(jnp.bfloat16)
    grad_queries = (
        jnp.einsum("hqk,khd->qhd", grad_scores, key_heads, preferred_element_type=jnp.float32)
        * score_scale
    )
    grad_keys = (
        jnp.einsum("hqk,qhd->khd", grad_scores, queries, preferred_element_type=jnp.float32)
        * score_scale
    )
    grad_values = jnp.einsum("hqk,qhd->khd", probs, grad_mixed, preferred_element_type=jnp.float32)
    grad_projected = jnp.concatenate(
        [
            grad_queries.reshape(seq_rows, model_width),
            grad_keys.reshape(seq_rows, model_width),
            grad_values.reshape(seq_rows, model_width),
        ],
        axis=1,
    ).astype(jnp.bfloat16)
    grad_qkv = inner_rows(hidden_one, grad_projected)
    grad_query_bias = column_sum(grad_projected[:, :model_width])
    grad_value_bias = column_sum(grad_projected[:, 2 * model_width :])
    grad_hidden_one = jnp.dot(grad_projected, qkv_weight.T, preferred_element_type=jnp.float32)
    grad_first_gain = jnp.sum(grad_hidden_one * normed_one, axis=0)
    grad_first_shift = jnp.sum(grad_hidden_one, axis=0)
    grad_input = (
        grad_mid + norm_back(grad_hidden_one * first_gain_f, normed_one, inverse_one)
    ).astype(jnp.bfloat16)
    weight_grads = [
        grad_qkv,
        grad_out,
        grad_fc,
        grad_proj,
        grad_first_gain,
        grad_first_shift,
        grad_query_bias,
        grad_value_bias,
        grad_out_bias,
        grad_second_gain,
        grad_second_shift,
        grad_fc_bias,
        grad_proj_bias,
    ]
    return (output_rows, grad_input, weight_grads)


def body(params, moment_one, moment_two, inputs, cotangent, segments, windows):
    gathered = lax.all_gather(params, "opt", axis=0, tiled=True)
    weights = unpack_weights(gathered, inputs.shape[2], FF)
    output_list = []
    input_list = []
    totals = None
    for micro_index in range(inputs.shape[0]):
        output_rows, grad_rows, weight_grads = sequence_pass(
            weights,
            inputs[micro_index],
            cotangent[micro_index],
            segments[micro_index],
            windows[micro_index],
        )
        output_list.append(output_rows)
        input_list.append(grad_rows)
        if totals is None:
            totals = weight_grads
        else:
            totals = [
                earlier_sum + later_sum for earlier_sum, later_sum in zip(totals, weight_grads)
            ]
    flat_total = jnp.concatenate([piece.reshape(-1) for piece in totals])
    opt_count = lax.axis_size("opt")
    dp_count = lax.axis_size("dp")
    blocks = (
        flat_total.reshape(opt_count, dp_count, -1)
        .transpose(1, 0, 2)
        .reshape(opt_count * dp_count, -1)
    )
    owned_piece = lax.psum_scatter(blocks, ("dp", "opt"), scatter_dimension=0, tiled=True)
    owned_grads = lax.all_gather(owned_piece, "dp", axis=0, tiled=True).reshape(-1)
    shard_length = params.shape[0]
    positions = lax.axis_index("opt") * shard_length + jnp.arange(shard_length, dtype=jnp.int32)
    decay_mask = (positions < MATRIX_PARAMS).astype(jnp.float32)
    old_values = params.astype(jnp.float32)
    first_moment = 0.5 * moment_one + 0.5 * owned_grads
    second_moment = 0.5 * moment_two + 0.5 * owned_grads * owned_grads
    update = (
        first_moment / (jnp.sqrt(second_moment) + 1e-08) + WEIGHT_DECAY * decay_mask * old_values
    )
    new_values = old_values - LEARN_RATE * update
    return (
        jnp.stack(output_list),
        jnp.stack(input_list),
        owned_grads,
        new_values,
        first_moment,
        second_moment,
        new_values.astype(jnp.bfloat16),
    )


def solution(mesh):
    placed = (
        P("opt"),
        P("opt"),
        P("opt"),
        P(("dp", "opt"), None, None),
        P(("dp", "opt"), None, None),
        P(("dp", "opt"), None),
        P(("dp", "opt")),
    )
    return jax.shard_map(
        body,
        mesh=mesh,
        in_specs=placed,
        out_specs=(
            P(("dp", "opt"), None, None),
            P(("dp", "opt"), None, None),
            P("opt"),
            P("opt"),
            P("opt"),
            P("opt"),
            P("opt"),
        ),
        check_vma=False,
    )
```

profile of v0, /device:TPU:0, one launch (start us, length us, event | category | flops | bytes accessed | tf_op | source)
XLA Modules:
  0.0 1707.5 jit_solution(409223282035159766)
XLA Ops:
  10.5 298.3 %all-gather.4.cloned.1.call-done = bf16[12595200]{0:T(1024)(128)(2,1)} async-done(((bf16[6297600]{0:T(1024)(128)(2,1)}), bf16[12595200]{0:T(1024)(128)(2,1)}) %all-gather.4.cloned.1.call-update) | async-done | bytes 25190416 | tf_op jit(solution)/shard_map/all_gather | solution.py:206
  308.8 6.4 slice.158
  315.2 10.3 slice.129
  337.9 11.4 fusion.105
  349.3 13.3 slice.146
  362.5 13.3 slice.143
  391.1 5.0 convolution_add_fusion
  399.3 6.6 convert_reduce_fusion
  405.9 4.2 fusion.113
  410.1 4.3 convert_reduce_fusion.1
  433.8 8.6 fusion.102
  442.4 8.8 fusion.72
  462.2 6.8 add_bitcast_fusion.2
  468.9 12.3 copy.96
  481.3 10.5 constant_dynamic-update-slice_fusion.11
  495.5 14.6 add_bitcast_fusion.1
  510.1 14.8 copy.98
  525.0 8.6 add_bitcast_fusion
  533.6 9.8 copy.99
  543.4 4.4 constant_dynamic-update-slice_fusion.10
  547.8 6.0 constant_dynamic-update-slice_fusion.9
  553.9 6.0 constant_dynamic-update-slice_fusion.8
  565.3 51.0 %reshape.377 = f32[2,16,393600]{2,1,0:T(8,128)} reshape(f32[12595200]{0:T(1024)} %constant_dynamic-update-slice_fusion) | data formatting | bytes 100761600 | tf_op jit(solution)/shard_map/reshape | solution.py:231
  616.2 68.9 %copy.87 = f32[16,2,393600]{2,1,0:T(2,128)} copy(f32[16,2,393600]{2,0,1:T(8,128)} %bitcast.212) | data formatting | bytes 100761600 | tf_op jit(solution)/shard_map/transpose | solution.py:232
  685.2 78.3 %reshape.378 = f32[32,393600]{1,0:T(8,128)} reshape(f32[16,2,393600]{2,1,0:T(2,128)} %copy.87) | data formatting | bytes 100761600 | tf_op jit(solution)/shard_map/reshape | solution.py:233
  763.6 721.8 %all-reduce.3.cloned.1.call-done = f32[32,393600]{1,0:T(8,128)} async-done(((f32[32,393600]{1,0:T(8,128)}), f32[32,393600]{1,0:T(8,128)}) %all-reduce.3.cloned.1.call-update) | async-done | bytes 50380816
  1485.4 6.6 dynamic-slice_bitcast_fusion
  1492.0 5.1 fusion.29
  1497.3 6.2 fusion.30
  1505.8 114.9 %all-gather.6.cloned.1.call-done = f32[16,1,393600]{2,1,0:T(1,128)} async-done(((f32[1,1,393600]{2,1,0:T(1,128)}), f32[16,1,393600]{2,1,0:T(1,128)}) %all-gather.6.cloned.1.call-update) | async-done | bytes 25190416 | tf_op jit(solution)/shard_map/all_gather | solution.py:236
  1620.7 61.1 %fusion.103 = (bf16[6297600]{0:T(1024)(128)(2,1)}, f32[6297600]{0:T(1024)}, f32[6297600]{0:T(1024)}, f32[6297600]{0:T(1024)}) fusion(s32[]{:T(128)S(6)} %mul.433, bf16[6297600]{0:T(1024)(128)(2,1)} %param.7, f32[6297600]{0:T(1024)} %bitcast.215, f32[6297600]{0:T(1024)} %param.9, f32[6297600]{0:T(1024)} %param.8), kind=kLoop, calls=%fused_computation.218 | loop fusion | flops 107059200 | bytes 176332800 | tf_op jit(solution)/shard_map/convert_element_type | solution.py:254
  1681.8 19.0 %copy.114 = f32[6297600]{0:T(1024)} copy(f32[6297600]{0:T(1024)} %bitcast.216) | data formatting | bytes 50380800
  (279 shorter events, 75.3 us)
Async XLA Ops:
  7.2 301.6 %all-gather.4.cloned.1.call-start = ((), (), s32[]{:S(2)}) async-start(), calls=%async_computation | async-start | bytes 37785600 | tf_op jit(solution)/shard_map/all_gather | solution.py:206
  7.9 1477.5 %all-reduce.3.cloned.1.call-start = ((), (), s32[]{:S(2)}) async-start(), calls=%async_computation.2 | async-start | bytes 100761600
  8.7 449.6 %copy-start.64 = (f32[128]{0:T(128)}, f32[128]{0:T(128)S(1)}, u32[]{:S(2)}) copy-start(f32[128]{0:T(128)S(1)} %get-tuple-element.90) | copy-start | bytes 1540
  8.7 453.4 %copy-start.62 = (f32[128]{0:T(128)}, f32[128]{0:T(128)S(1)}, u32[]{:S(2)}) copy-start(f32[128]{0:T(128)S(1)} %get-tuple-element.89) | copy-start | bytes 1540
  9.0 453.1 %copy-start.66 = (f32[128]{0:T(128)}, f32[128]{0:T(128)S(1)}, u32[]{:S(2)}) copy-start(f32[128]{0:T(128)S(1)} %add_rsqrt_fusion.1) | copy-start | bytes 1540
  9.1 449.3 %copy-start.68 = (f32[128]{0:T(128)}, f32[128]{0:T(128)S(1)}, u32[]{:S(2)}) copy-start(f32[128]{0:T(128)S(1)} %add_rsqrt_fusion.3) | copy-start | bytes 1540
  326.8 135.4 %copy-start.52 = (f32[1024]{0:T(1024)}, f32[1024]{0:T(1024)S(1)}, u32[]{:S(2)}) copy-start(f32[1024]{0:T(1024)S(1)} %get-tuple-element.46) | copy-start | bytes 12292
  330.9 44.9 %copy-start.34 = (bf16[128,1024]{0,1:T(8,128)(2,1)}, bf16[128,1024]{0,1:T(8,128)(2,1)S(1)}, u32[]{:S(2)}) copy-start(bf16[128,1024]{0,1:T(8,128)(2,1)S(1)} %copy.75) | copy-start | bytes 786436
  389.8 27.8 %copy-start.7 = (f32[128,1024]{1,0:T(8,128)}, f32[128,1024]{1,0:T(8,128)S(1)}, u32[]{:S(2)}) copy-start(f32[128,1024]{1,0:T(8,128)S(1)} %get-tuple-element.78) | copy-start | bytes 1572868
  399.3 10.8 copy-start.17
  433.8 8.6 copy-start.18
  433.8 8.6 copy-start.46
  433.8 20.4 %slice-start.8 = ((s8[6291456]{0:T(1024)(128)(4,1)}), s8[4194304]{0:T(1024)(128)(4,1)S(1)}, s32[]{:S(2)}) async-start(s8[6291456]{0:T(1024)(128)(4,1)} %bitcast.223), calls=%async_computation.11 | async-start | bytes 8388608
  442.4 9.5 copy-start.29
  442.4 11.7 slice-start.9
  442.4 11.7 copy-start.48
  481.3 10.5 copy-start.21
  481.3 10.5 copy-start.41
  495.5 29.4 %slice-start.2 = ((s8[16777216]{0:T(1024)(128)(4,1)}), s8[4194304]{0:T(1024)(128)(4,1)S(1)}, s32[]{:S(2)}) async-start(s8[16777216]{0:T(1024)(128)(4,1)} %bitcast.213), calls=%async_computation.5 | async-start | bytes 8388608
  495.5 29.4 %slice-start.3 = ((s8[16777216]{0:T(1024)(128)(4,1)}), s8[4194304]{0:T(1024)(128)(4,1)S(1)}, s32[]{:S(2)}) async-start(s8[16777216]{0:T(1024)(128)(4,1)} %bitcast.213), calls=%async_computation.6 | async-start | bytes 8388608
  495.5 29.4 %slice-start.4 = ((s8[16777216]{0:T(1024)(128)(4,1)}), s8[4194304]{0:T(1024)(128)(4,1)S(1)}, s32[]{:S(2)}) async-start(s8[16777216]{0:T(1024)(128)(4,1)} %bitcast.213), calls=%async_computation.7 | async-start | bytes 8388608
  510.1 14.8 slice-start.5
  510.1 14.8 copy-start.11
  510.1 14.9 copy-start.47
  533.6 14.2 copy-start
  553.9 8.4 copy-start.54
  553.9 8.4 copy-start.55
  553.9 10.2 copy-start.60
  553.9 10.2 copy-start.61
  763.5 857.2 %all-gather.6.cloned.1.call-start = ((), (), s32[]{:S(2)}) async-start(), calls=%async_computation.1 | async-start | bytes 26764800 | tf_op jit(solution)/shard_map/all_gather | solution.py:236
  763.6 728.5 %copy-start.6 = (f32[128,1024]{1,0:T(8,128)S(1)}, f32[128,1024]{1,0:T(8,128)}, u32[]{:S(2)}) copy-start(f32[128,1024]{1,0:T(8,128)} %copy-done.3) | copy-start | bytes 1572868
  763.6 728.5 %copy-start.74 = (f32[1024]{0:T(1024)S(1)}, f32[1024]{0:T(1024)}, u32[]{:S(2)}) copy-start(f32[1024]{0:T(1024)} %get-tuple-element.40) | copy-start | bytes 12292
  (62 other events, 252.2 us)
Sparse Core Ops, SparseCore 0:
  9.6 299.1 all-gather.3
  763.6 721.7 all-reduce.2
  1492.1 128.5 all-gather.5
where the time goes:
time: 1720 us; the launch traced here: 1710 us
  waiting for transfers between devices  1140 us (66%)
  local copies, waits for them, and re-layouts  364 us (21%)
  matrix products  114 us (7%)
  other arithmetic  78.9 us (5%)
    unnamed x4, waiting for transfers between devices  723 us
    all_gather x1, waiting for transfers between devices, body(): gathered = lax.all_gather(params, 'opt', axis=0, tiled=True)  298 us
    all_gather x1, waiting for transfers between devices, body(): lax.all_gather(owned_piece, 'dp', axis=0, tiled=True).reshape(-1)  115 us
    unnamed x192, local copies, waits for them, and re-layouts  97.4 us
    reshape x1, local copies, waits for them, and re-layouts, body(): blocks = flat_total.reshape(opt_count, dp_count, -1).transpose(1, 0, 2).r...  78.3 us
    transpose x1, local copies, waits for them, and re-layouts, body(): blocks = flat_total.reshape(opt_count, dp_count, -1).transpose(1, 0, 2).r...  68.9 us
    convert_element_type x1, other arithmetic, body(): new_values.astype(jnp.bfloat16)  61.1 us
    slice x7, local copies, waits for them, and re-layouts, unpack_weights(): pieces.append(flat_values[position:position + amount].reshape(piece_dims))  60.5 us
  transfers between devices with their start and end apart: 3, of which 3 were waited for; matrix products, arithmetic and copies ran while one was open for 1% of the time, Pallas kernels for 0%

commit v1 on v0

--- a/solution.py
+++ b/solution.py
@@ -11,6 +11,22 @@
 GELU_C = math.sqrt(2.0 / math.pi)
 LEARN_RATE = 0.01
 WEIGHT_DECAY = 0.1
+
+
+def gather_around(x, axis, dim):
+    ways, here, step = (lax.axis_size(axis), lax.axis_index(axis), x.shape[dim])
+    shape = [n * ways if d == dim else n for d, n in enumerate(x.shape)]
+    full = lax.dynamic_update_slice_in_dim(jnp.zeros(shape, x.dtype), x, here * step, axis=dim)
+    going_up = going_down = x
+    for far in range(1, ways // 2 + 1):
+        going_up = lax.ppermute(going_up, axis, [(d, (d + 1) % ways) for d in range(ways)])
+        full = lax.dynamic_update_slice_in_dim(full, going_up, (here - far) % ways * step, axis=dim)
+        if 2 * far < ways:
+            going_down = lax.ppermute(going_down, axis, [(d, (d - 1) % ways) for d in range(ways)])
+            full = lax.dynamic_update_slice_in_dim(
+                full, going_down, (here + far) % ways * step, axis=dim
+            )
+    return full
 
 
 def unpack_weights(flat_values, model_width, hidden_units):
@@ -233,7 +249,7 @@
         .reshape(opt_count * dp_count, -1)
     )
     owned_piece = lax.psum_scatter(blocks, ("dp", "opt"), scatter_dimension=0, tiled=True)
-    owned_grads = lax.all_gather(owned_piece, "dp", axis=0, tiled=True).reshape(-1)
+    owned_grads = gather_around(owned_piece, "dp", 0).reshape(-1)
     shard_length = params.shape[0]
     positions = lax.axis_index("opt") * shard_length + jnp.arange(shard_length, dtype=jnp.int32)
     decay_mask = (positions < MATRIX_PARAMS).astype(jnp.float32)

time: 1720 us -> 2370 us (1.38)
  local copies, waits for them, and re-layouts: 364 us -> 863 us
  starting transfers between devices: 0.12 us -> 208 us
  waiting for transfers between devices: 1140 us -> 1060 us
    dynamic_update_slice x0 -> x16, local copies, waits for them, and re-layouts: none -> 486 us  [the longest x8 243 us: gather_around(): lax.dynamic_update_slice_in_dim(full, going_up, (here - far) % ways * ste...]
    ppermute x0 -> x15, starting transfers between devices: none -> 208 us  [the longest x8 204 us: gather_around(): lax.ppermute(going_up, axis, [(d, (d + 1) % ways) for d in range(ways)])]
    all_gather x1 -> x0, waiting for transfers between devices: 115 us -> none  [body(): lax.all_gather(owned_piece, 'dp', axis=0, tiled=True).reshape(-1)]
    ppermute x0 -> x15, waiting for transfers between devices: none -> 41 us  [the longest x8 41 us: gather_around(): lax.ppermute(going_up, axis, [(d, (d + 1) % ways) for d in range(ways)])]
    unnamed x192 -> x259, local copies, waits for them, and re-layouts: 97.4 us -> 78.8 us
    unnamed x4 -> x3, waiting for transfers between devices: 723 us -> 723 us
  transfers between devices with their start and end apart: 3 -> 17, of which waited for: 3 -> 9; matrix products, arithmetic and copies ran while one was open for 1% -> 20% of each run, Pallas kernels for 0% -> 0%
where the time goes in v1:
time: 2370 us; the launch traced here: 2350 us
  waiting for transfers between devices  1060 us (45%)
  local copies, waits for them, and re-layouts  863 us (36%)
  starting transfers between devices  208 us (9%)
  matrix products  115 us (5%)
  other arithmetic  82 us (3%)
    unnamed x3, waiting for transfers between devices  723 us
    all_gather x1, waiting for transfers between devices, body(): gathered = lax.all_gather(params, 'opt', axis=0, tiled=True)  298 us
    dynamic_update_slice x8, local copies, waits for them, and re-layouts, gather_around(): lax.dynamic_update_slice_in_dim(full, going_up, (here - far) % ways * ste...  243 us
    dynamic_update_slice x7, local copies, waits for them, and re-layouts, gather_around(): lax.dynamic_update_slice_in_dim(full, going_down, (here + far) % ways * s...  213 us
    ppermute x8, starting transfers between devices, gather_around(): lax.ppermute(going_up, axis, [(d, (d + 1) % ways) for d in range(ways)])  204 us
    unnamed x259, local copies, waits for them, and re-layouts  78.8 us
    reshape x1, local copies, waits for them, and re-layouts, body(): blocks = flat_total.reshape(opt_count, dp_count, -1).transpose(1, 0, 2).r...  78.7 us
    transpose x1, local copies, waits for them, and re-layouts, body(): blocks = flat_total.reshape(opt_count, dp_count, -1).transpose(1, 0, 2).r...  68.9 us
  transfers between devices with their start and end apart: 17, of which 9 were waited for; matrix products, arithmetic and copies ran while one was open for 20% of the time, Pallas kernels for 0%

profile of v1, /device:TPU:0, one launch (start us, length us, event | category | flops | bytes accessed | tf_op | source)
XLA Modules:
  0.0 2345.1 jit_solution(2070826129808236557)
XLA Ops:
  10.5 298.3 %all-gather.2.cloned.1.call-done = bf16[12595200]{0:T(1024)(128)(2,1)} async-done(((bf16[6297600]{0:T(1024)(128)(2,1)}), bf16[12595200]{0:T(1024)(128)(2,1)}) %all-gather.2.cloned.1.call-update) | async-done | bytes 25190416 | tf_op jit(solution)/shard_map/all_gather | solution.py:222
  353.7 13.3 slice.143
  466.6 14.3 copy.98
  572.1 50.8 %reshape.377 = f32[2,16,393600]{2,1,0:T(8,128)} reshape(f32[12595200]{0:T(1024)} %constant_dynamic-update-slice_fusion) | data formatting | bytes 100761600 | tf_op jit(solution)/shard_map/reshape | solution.py:247
  622.9 68.9 %copy.87 = f32[16,2,393600]{2,1,0:T(2,128)} copy(f32[16,2,393600]{2,0,1:T(8,128)} %bitcast.209) | data formatting | bytes 100761600 | tf_op jit(solution)/shard_map/transpose | solution.py:248
  691.8 78.7 %reshape.378 = f32[32,393600]{1,0:T(8,128)} reshape(f32[16,2,393600]{2,1,0:T(2,128)} %copy.87) | data formatting | bytes 100761600 | tf_op jit(solution)/shard_map/reshape | solution.py:249
  770.6 721.9 %all-reduce.3.cloned.1.call-done = f32[32,393600]{1,0:T(8,128)} async-done(((f32[32,393600]{1,0:T(8,128)}), f32[32,393600]{1,0:T(8,128)}) %all-reduce.3.cloned.1.call-update) | async-done | bytes 50380816
  1502.5 18.2 collective-permute-done
  1543.4 26.2 %collective-permute-start.4 = (f32[1,393600]{1,0:T(1,128)S(1)}, f32[1,393600]{1,0:T(1,128)S(1)}, u32[]{:S(2)}, u32[]{:S(2)}) collective-permute-start(f32[1,393600]{1,0:T(1,128)S(1)} %collective-permute-done.2), channel_id=1, source_target_pairs={{0,2},{2,4},{4,6},{6,8},{8,10},{10,12},{12,14},{14,16},{16,18},{18... | collective-permute-start | bytes 4723208 | tf_op jit(solution)/shard_map/ppermute | solution.py:22
  1572.6 32.9 %collective-permute-start.6 = (f32[1,393600]{1,0:T(1,128)S(1)}, f32[1,393600]{1,0:T(1,128)S(1)}, u32[]{:S(2)}, u32[]{:S(2)}) collective-permute-start(f32[1,393600]{1,0:T(1,128)S(1)} %collective-permute-done.4), channel_id=1, source_target_pairs={{0,2},{2,4},{4,6},{6,8},{8,10},{10,12},{12,14},{14,16},{16,18},{18... | collective-permute-start | bytes 4723208 | tf_op jit(solution)/shard_map/ppermute | solution.py:22
  1608.6 32.0 %collective-permute-start.8 = (f32[1,393600]{1,0:T(1,128)S(1)}, f32[1,393600]{1,0:T(1,128)S(1)}, u32[]{:S(2)}, u32[]{:S(2)}) collective-permute-start(f32[1,393600]{1,0:T(1,128)S(1)} %collective-permute-done.6), channel_id=1, source_target_pairs={{0,2},{2,4},{4,6},{6,8},{8,10},{10,12},{12,14},{14,16},{16,18},{18... | collective-permute-start | bytes 4723208 | tf_op jit(solution)/shard_map/ppermute | solution.py:22
  1643.6 33.0 %collective-permute-start.10 = (f32[1,393600]{1,0:T(1,128)S(1)}, f32[1,393600]{1,0:T(1,128)}, u32[]{:S(2)}, u32[]{:S(2)}) collective-permute-start(f32[1,393600]{1,0:T(1,128)S(1)} %collective-permute-done.8), channel_id=1, source_target_pairs={{0,2},{2,4},{4,6},{6,8},{8,10},{10,12},{12,14},{14,16},{16,18},{18... | collective-permute-start | bytes 4723208 | tf_op jit(solution)/shard_map/ppermute | solution.py:22
  1679.8 32.7 %collective-permute-start.12 = (f32[1,393600]{1,0:T(1,128)}, f32[1,393600]{1,0:T(1,128)}, u32[]{:S(2)}, u32[]{:S(2)}) collective-permute-start(f32[1,393600]{1,0:T(1,128)} %collective-permute-done.10), channel_id=1, source_target_pairs={{0,2},{2,4},{4,6},{6,8},{8,10},{10,12},{12,14},{14,16},{16,18},{18... | collective-permute-start | bytes 4723208 | tf_op jit(solution)/shard_map/ppermute | solution.py:22
  1715.8 34.0 %collective-permute-start.14 = (f32[1,393600]{1,0:T(1,128)}, f32[1,393600]{1,0:T(1,128)}, u32[]{:S(2)}, u32[]{:S(2)}) collective-permute-start(f32[1,393600]{1,0:T(1,128)} %collective-permute-done.12), channel_id=1, source_target_pairs={{0,2},{2,4},{4,6},{6,8},{8,10},{10,12},{12,14},{14,16},{16,18},{18... | collective-permute-start | bytes 4723208 | tf_op jit(solution)/shard_map/ppermute | solution.py:22
  1770.3 30.4 %dynamic_update_slice.48 = f32[16,393600]{1,0:T(8,128)} dynamic-update-slice(f32[16,393600]{1,0:T(8,128)} %broadcast_in_dim.31, f32[1,393600]{1,0:T(1,128)S(1)} %copy-done.26, s32[]{:T(128)S(6)} %select_n.122, s32[]{:T(128)} %constant.138.clone.1) | dynamic-update-slice | bytes 3148804 | tf_op jit(solution)/shard_map/dynamic_update_slice | solution.py:19
  1800.7 30.4 %dynamic_update_slice.49 = f32[16,393600]{1,0:T(8,128)} dynamic-update-slice(f32[16,393600]{1,0:T(8,128)} %dynamic_update_slice.48, f32[1,393600]{1,0:T(1,128)S(1)} %copy-done.48, s32[]{:T(128)S(6)} %select_n.124, s32[]{:T(128)} %constant.138.clone.1) | dynamic-update-slice | bytes 3148804 | tf_op jit(solution)/shard_map/dynamic_update_slice | solution.py:23
  1831.1 30.4 %dynamic_update_slice.50 = f32[16,393600]{1,0:T(8,128)} dynamic-update-slice(f32[16,393600]{1,0:T(8,128)} %dynamic_update_slice.49, f32[1,393600]{1,0:T(1,128)S(1)} %copy-done.50, s32[]{:T(128)S(6)} %select_n.126, s32[]{:T(128)} %constant.138.clone.1) | dynamic-update-slice | bytes 3148804 | tf_op jit(solution)/shard_map/dynamic_update_slice | solution.py:26
  1861.5 30.4 %dynamic_update_slice.51 = f32[16,393600]{1,0:T(8,128)} dynamic-update-slice(f32[16,393600]{1,0:T(8,128)} %dynamic_update_slice.50, f32[1,393600]{1,0:T(1,128)S(1)} %copy-done.52, s32[]{:T(128)S(6)} %select_n.128, s32[]{:T(128)} %constant.138.clone.1) | dynamic-update-slice | bytes 3148804 | tf_op jit(solution)/shard_map/dynamic_update_slice | solution.py:23
  1891.9 30.4 %dynamic_update_slice.52 = f32[16,393600]{1,0:T(8,128)} dynamic-update-slice(f32[16,393600]{1,0:T(8,128)} %dynamic_update_slice.51, f32[1,393600]{1,0:T(1,128)S(1)} %copy-done.54, s32[]{:T(128)S(6)} %select_n.130, s32[]{:T(128)} %constant.138.clone.1) | dynamic-update-slice | bytes 3148804 | tf_op jit(solution)/shard_map/dynamic_update_slice | solution.py:26
  1922.2 30.4 %dynamic_update_slice.53 = f32[16,393600]{1,0:T(8,128)} dynamic-update-slice(f32[16,393600]{1,0:T(8,128)} %dynamic_update_slice.52, f32[1,393600]{1,0:T(1,128)S(1)} %copy-done.56, s32[]{:T(128)S(6)} %select_n.132, s32[]{:T(128)} %constant.138.clone.1) | dynamic-update-slice | bytes 3148804 | tf_op jit(solution)/shard_map/dynamic_update_slice | solution.py:23
  1952.6 30.4 %dynamic_update_slice.54 = f32[16,393600]{1,0:T(8,128)} dynamic-update-slice(f32[16,393600]{1,0:T(8,128)} %dynamic_update_slice.53, f32[1,393600]{1,0:T(1,128)S(1)} %copy-done.58, s32[]{:T(128)S(6)} %select_n.134, s32[]{:T(128)} %constant.138.clone.1) | dynamic-update-slice | bytes 3148804 | tf_op jit(solution)/shard_map/dynamic_update_slice | solution.py:26
  1983.0 30.4 %dynamic_update_slice.55 = f32[16,393600]{1,0:T(8,128)} dynamic-update-slice(f32[16,393600]{1,0:T(8,128)} %dynamic_update_slice.54, f32[1,393600]{1,0:T(1,128)S(1)} %copy-done.60, s32[]{:T(128)S(6)} %select_n.136, s32[]{:T(128)} %constant.138.clone.1) | dynamic-update-slice | bytes 3148804 | tf_op jit(solution)/shard_map/dynamic_update_slice | solution.py:23
  2013.4 30.4 %dynamic_update_slice.56 = f32[16,393600]{1,0:T(8,128)} dynamic-update-slice(f32[16,393600]{1,0:T(8,128)} %dynamic_update_slice.55, f32[1,393600]{1,0:T(1,128)S(1)} %copy-done.62, s32[]{:T(128)S(6)} %select_n.138, s32[]{:T(128)} %constant.138.clone.1) | dynamic-update-slice | bytes 3148804 | tf_op jit(solution)/shard_map/dynamic_update_slice | solution.py:26
  2043.8 30.3 %dynamic_update_slice.57 = f32[16,393600]{1,0:T(8,128)} dynamic-update-slice(f32[16,393600]{1,0:T(8,128)} %dynamic_update_slice.56, f32[1,393600]{1,0:T(1,128)S(1)} %copy-done.64, s32[]{:T(128)S(6)} %select_n.140, s32[]{:T(128)} %constant.138.clone.1) | dynamic-update-slice | bytes 3148804 | tf_op jit(solution)/shard_map/dynamic_update_slice | solution.py:23
  2074.0 30.4 %dynamic_update_slice.58 = f32[16,393600]{1,0:T(8,128)} dynamic-update-slice(f32[16,393600]{1,0:T(8,128)} %dynamic_update_slice.57, f32[1,393600]{1,0:T(1,128)} %collective-permute-done.9, s32[]{:T(128)S(6)} %select_n.142, s32[]{:T(128)} %constant.138.clone.1) | dynamic-update-slice | bytes 3148804 | tf_op jit(solution)/shard_map/dynamic_update_slice | solution.py:26
  2104.4 30.4 %dynamic_update_slice.59 = f32[16,393600]{1,0:T(8,128)} dynamic-update-slice(f32[16,393600]{1,0:T(8,128)} %dynamic_update_slice.58, f32[1,393600]{1,0:T(1,128)} %collective-permute-done.10, s32[]{:T(128)S(6)} %select_n.144, s32[]{:T(128)} %constant.138.clone.1) | dynamic-update-slice | bytes 3148804 | tf_op jit(solution)/shard_map/dynamic_update_slice | solution.py:23
  2134.8 30.4 %dynamic_update_slice.60 = f32[16,393600]{1,0:T(8,128)} dynamic-update-slice(f32[16,393600]{1,0:T(8,128)} %dynamic_update_slice.59, f32[1,393600]{1,0:T(1,128)} %collective-permute-done.11, s32[]{:T(128)S(6)} %select_n.146, s32[]{:T(128)} %constant.138.clone.1) | dynamic-update-slice | bytes 3148804 | tf_op jit(solution)/shard_map/dynamic_update_slice | solution.py:26
  2165.2 30.4 %dynamic_update_slice.61 = f32[16,393600]{1,0:T(8,128)} dynamic-update-slice(f32[16,393600]{1,0:T(8,128)} %dynamic_update_slice.60, f32[1,393600]{1,0:T(1,128)} %collective-permute-done.12, s32[]{:T(128)S(6)} %select_n.148, s32[]{:T(128)} %constant.138.clone.1) | dynamic-update-slice | bytes 3148804 | tf_op jit(solution)/shard_map/dynamic_update_slice | solution.py:23
  2195.6 30.4 %dynamic_update_slice.62 = f32[16,393600]{1,0:T(8,128)} dynamic-update-slice(f32[16,393600]{1,0:T(8,128)} %dynamic_update_slice.61, f32[1,393600]{1,0:T(1,128)} %collective-permute-done.13, s32[]{:T(128)S(6)} %select_n.150, s32[]{:T(128)} %constant.138.clone.1) | dynamic-update-slice | bytes 3148804 | tf_op jit(solution)/shard_map/dynamic_update_slice | solution.py:26
  2226.0 30.4 %dynamic_update_slice.63 = f32[16,393600]{1,0:T(8,128)} dynamic-update-slice(f32[16,393600]{1,0:T(8,128)} %dynamic_update_slice.62, f32[1,393600]{1,0:T(1,128)} %collective-permute-done.14, s32[]{:T(128)S(6)} %select_n.152, s32[]{:T(128)} %constant.138.clone.1) | dynamic-update-slice | bytes 3148804 | tf_op jit(solution)/shard_map/dynamic_update_slice | solution.py:23
  2256.4 20.3 reshape.379
  2276.7 61.2 %fusion.103 = (bf16[6297600]{0:T(1024)(128)(2,1)}, f32[6297600]{0:T(1024)}, f32[6297600]{0:T(1024)}, f32[6297600]{0:T(1024)}) fusion(s32[]{:T(128)S(6)} %mul.433, bf16[6297600]{0:T(1024)(128)(2,1)} %param.7, f32[6297600]{0:T(1024)} %reshape.379, f32[6297600]{0:T(1024)} %param.9, f32[6297600]{0:T(1024)} %param.8), kind=kLoop, calls=%fused_computation.218 | loop fusion | flops 107059200 | bytes 176332800 | tf_op jit(solution)/shard_map/convert_element_type | solution.py:270
  (394 shorter events, 306.6 us)
Async XLA Ops:
  7.2 301.6 %all-gather.2.cloned.1.call-start = ((), (), s32[]{:S(2)}) async-start(), calls=%async_computation | async-start | bytes 37785600 | tf_op jit(solution)/shard_map/all_gather | solution.py:222
  7.9 1484.5 %all-reduce.3.cloned.1.call-start = ((), (), s32[]{:S(2)}) async-start(), calls=%async_computation.1 | async-start | bytes 100761600
  8.7 318.1 %copy-start.82 = (f32[128]{0:T(128)}, f32[128]{0:T(128)S(1)}, u32[]{:S(2)}) copy-start(f32[128]{0:T(128)S(1)} %get-tuple-element.90) | copy-start | bytes 1540
  8.7 391.1 %copy-start.78 = (f32[128]{0:T(128)}, f32[128]{0:T(128)S(1)}, u32[]{:S(2)}) copy-start(f32[128]{0:T(128)S(1)} %get-tuple-element.89) | copy-start | bytes 1540
  9.1 390.8 %copy-start.90 = (f32[128]{0:T(128)}, f32[128]{0:T(128)S(1)}, u32[]{:S(2)}) copy-start(f32[128]{0:T(128)S(1)} %add_rsqrt_fusion.1) | copy-start | bytes 1540
  770.5 942.0 %copy-start.104 = (f32[128]{0:T(128)S(1)}, f32[128]{0:T(128)}, u32[]{:S(2)}) copy-start(f32[128]{0:T(128)} %get-tuple-element.15) | copy-start | bytes 1540
  770.5 942.0 %copy-start.103 = (f32[128]{0:T(128)S(1)}, f32[128]{0:T(128)}, u32[]{:S(2)}) copy-start(f32[128]{0:T(128)} %get-tuple-element.17) | copy-start | bytes 1540
  770.5 942.0 %copy-start.102 = (f32[128]{0:T(128)S(1)}, f32[128]{0:T(128)}, u32[]{:S(2)}) copy-start(f32[128]{0:T(128)} %get-tuple-element.14) | copy-start | bytes 1540
  770.5 942.0 %copy-start.101 = (f32[128]{0:T(128)S(1)}, f32[128]{0:T(128)}, u32[]{:S(2)}) copy-start(f32[128]{0:T(128)} %get-tuple-element.18) | copy-start | bytes 1540
  770.5 942.0 %copy-start.17 = (bf16[2,128,1024]{2,1,0:T(8,128)(2,1)S(1)}, bf16[2,128,1024]{2,1,0:T(8,128)(2,1)}, u32[]{:S(2)}) copy-start(bf16[2,128,1024]{2,1,0:T(8,128)(2,1)} %param.10) | copy-start | bytes 1572868
  770.5 942.0 %copy-start.81 = (f32[128]{0:T(128)S(1)}, f32[128]{0:T(128)}, u32[]{:S(2)}) copy-start(f32[128]{0:T(128)} %copy-done.78) | copy-start | bytes 1540
  770.5 942.0 %copy-start.85 = (f32[128]{0:T(128)S(1)}, f32[128]{0:T(128)}, u32[]{:S(2)}) copy-start(f32[128]{0:T(128)} %copy-done.82) | copy-start | bytes 1540
  770.5 942.0 %copy-start.89 = (f32[128]{0:T(128)S(1)}, f32[128]{0:T(128)}, u32[]{:S(2)}) copy-start(f32[128]{0:T(128)} %copy-done.86) | copy-start | bytes 1540
  770.5 942.0 %copy-start.93 = (f32[128]{0:T(128)S(1)}, f32[128]{0:T(128)}, u32[]{:S(2)}) copy-start(f32[128]{0:T(128)} %copy-done.90) | copy-start | bytes 1540
  770.5 980.1 %copy-start.8 = (f32[128,1024]{1,0:T(8,128)S(1)}, f32[128,1024]{1,0:T(8,128)}, u32[]{:S(2)}) copy-start(f32[128,1024]{1,0:T(8,128)} %copy-done.5) | copy-start | bytes 1572868
  770.6 980.1 %copy-start.20 = (f32[128,4096]{1,0:T(8,128)S(1)}, f32[128,4096]{1,0:T(8,128)}, u32[]{:S(2)}) copy-start(f32[128,4096]{1,0:T(8,128)} %copy-done.18) | copy-start | bytes 6291460
  770.6 980.1 %copy-start.98 = (f32[1024]{0:T(1024)S(1)}, f32[1024]{0:T(1024)}, u32[]{:S(2)}) copy-start(f32[1024]{0:T(1024)} %get-tuple-element.40) | copy-start | bytes 12292
  1498.0 22.7 collective-permute-start
  1499.1 34.8 %collective-permute-start.1 = (f32[1,393600]{1,0:T(1,128)S(1)}, f32[1,393600]{1,0:T(1,128)S(1)}, u32[]{:S(2)}, u32[]{:S(2)}) collective-permute-start(f32[1,393600]{1,0:T(1,128)S(1)} %constant_dynamic-slice_fusion), channel_id=1, source_target_pairs={{0,30},{2,0},{4,2},{6,4},{8,6},{10,8},{12,10},{14,12},{16,14},{18,... | collective-permute-start | bytes 4723208 | tf_op jit(solution)/shard_map/ppermute | solution.py:25
  1520.7 22.7 collective-permute-start.2
  1533.9 35.7 %collective-permute-start.3 = (f32[1,393600]{1,0:T(1,128)S(1)}, f32[1,393600]{1,0:T(1,128)S(1)}, u32[]{:S(2)}, u32[]{:S(2)}) collective-permute-start(f32[1,393600]{1,0:T(1,128)S(1)} %collective-permute-done.1), channel_id=1, source_target_pairs={{0,30},{2,0},{4,2},{6,4},{8,6},{10,8},{12,10},{14,12},{16,14},{18,... | collective-permute-start | bytes 4723208 | tf_op jit(solution)/shard_map/ppermute | solution.py:25
  1543.4 29.3 %collective-permute-start.4 = (f32[1,393600]{1,0:T(1,128)S(1)}, f32[1,393600]{1,0:T(1,128)S(1)}, u32[]{:S(2)}, u32[]{:S(2)}) collective-permute-start(f32[1,393600]{1,0:T(1,128)S(1)} %collective-permute-done.2), channel_id=1, source_target_pairs={{0,2},{2,4},{4,6},{6,8},{8,10},{10,12},{12,14},{14,16},{16,18},{18... | collective-permute-start | bytes 4723208 | tf_op jit(solution)/shard_map/ppermute | solution.py:22
  1569.6 35.9 %collective-permute-start.5 = (f32[1,393600]{1,0:T(1,128)S(1)}, f32[1,393600]{1,0:T(1,128)S(1)}, u32[]{:S(2)}, u32[]{:S(2)}) collective-permute-start(f32[1,393600]{1,0:T(1,128)S(1)} %collective-permute-done.3), channel_id=1, source_target_pairs={{0,30},{2,0},{4,2},{6,4},{8,6},{10,8},{12,10},{14,12},{16,14},{18,... | collective-permute-start | bytes 4723208 | tf_op jit(solution)/shard_map/ppermute | solution.py:25
  1572.6 35.9 %collective-permute-start.6 = (f32[1,393600]{1,0:T(1,128)S(1)}, f32[1,393600]{1,0:T(1,128)S(1)}, u32[]{:S(2)}, u32[]{:S(2)}) collective-permute-start(f32[1,393600]{1,0:T(1,128)S(1)} %collective-permute-done.4), channel_id=1, source_target_pairs={{0,2},{2,4},{4,6},{6,8},{8,10},{10,12},{12,14},{14,16},{16,18},{18... | collective-permute-start | bytes 4723208 | tf_op jit(solution)/shard_map/ppermute | solution.py:22
  1605.5 35.1 %collective-permute-start.7 = (f32[1,393600]{1,0:T(1,128)S(1)}, f32[1,393600]{1,0:T(1,128)S(1)}, u32[]{:S(2)}, u32[]{:S(2)}) collective-permute-start(f32[1,393600]{1,0:T(1,128)S(1)} %collective-permute-done.5), channel_id=1, source_target_pairs={{0,30},{2,0},{4,2},{6,4},{8,6},{10,8},{12,10},{14,12},{16,14},{18,... | collective-permute-start | bytes 4723208 | tf_op jit(solution)/shard_map/ppermute | solution.py:25
  1608.6 35.1 %collective-permute-start.8 = (f32[1,393600]{1,0:T(1,128)S(1)}, f32[1,393600]{1,0:T(1,128)S(1)}, u32[]{:S(2)}, u32[]{:S(2)}) collective-permute-start(f32[1,393600]{1,0:T(1,128)S(1)} %collective-permute-done.6), channel_id=1, source_target_pairs={{0,2},{2,4},{4,6},{6,8},{8,10},{10,12},{12,14},{14,16},{16,18},{18... | collective-permute-start | bytes 4723208 | tf_op jit(solution)/shard_map/ppermute | solution.py:22
  1640.6 36.0 %collective-permute-start.9 = (f32[1,393600]{1,0:T(1,128)S(1)}, f32[1,393600]{1,0:T(1,128)}, u32[]{:S(2)}, u32[]{:S(2)}) collective-permute-start(f32[1,393600]{1,0:T(1,128)S(1)} %collective-permute-done.7), channel_id=1, source_target_pairs={{0,30},{2,0},{4,2},{6,4},{8,6},{10,8},{12,10},{14,12},{16,14},{18,... | collective-permute-start | bytes 4723208 | tf_op jit(solution)/shard_map/ppermute | solution.py:25
  1643.6 36.1 %collective-permute-start.10 = (f32[1,393600]{1,0:T(1,128)S(1)}, f32[1,393600]{1,0:T(1,128)}, u32[]{:S(2)}, u32[]{:S(2)}) collective-permute-start(f32[1,393600]{1,0:T(1,128)S(1)} %collective-permute-done.8), channel_id=1, source_target_pairs={{0,2},{2,4},{4,6},{6,8},{8,10},{10,12},{12,14},{14,16},{16,18},{18... | collective-permute-start | bytes 4723208 | tf_op jit(solution)/shard_map/ppermute | solution.py:22
  1676.6 37.9 %collective-permute-start.11 = (f32[1,393600]{1,0:T(1,128)}, f32[1,393600]{1,0:T(1,128)}, u32[]{:S(2)}, u32[]{:S(2)}) collective-permute-start(f32[1,393600]{1,0:T(1,128)} %collective-permute-done.9), channel_id=1, source_target_pairs={{0,30},{2,0},{4,2},{6,4},{8,6},{10,8},{12,10},{14,12},{16,14},{18,... | collective-permute-start | bytes 4723208 | tf_op jit(solution)/shard_map/ppermute | solution.py:25
  1679.8 36.1 %collective-permute-start.12 = (f32[1,393600]{1,0:T(1,128)}, f32[1,393600]{1,0:T(1,128)}, u32[]{:S(2)}, u32[]{:S(2)}) collective-permute-start(f32[1,393600]{1,0:T(1,128)} %collective-permute-done.10), channel_id=1, source_target_pairs={{0,2},{2,4},{4,6},{6,8},{8,10},{10,12},{12,14},{14,16},{16,18},{18... | collective-permute-start | bytes 4723208 | tf_op jit(solution)/shard_map/ppermute | solution.py:22
  1714.5 481.1 %collective-permute-start.13 = (f32[1,393600]{1,0:T(1,128)}, f32[1,393600]{1,0:T(1,128)}, u32[]{:S(2)}, u32[]{:S(2)}) collective-permute-start(f32[1,393600]{1,0:T(1,128)} %collective-permute-done.11), channel_id=1, source_target_pairs={{0,30},{2,0},{4,2},{6,4},{8,6},{10,8},{12,10},{14,12},{16,14},{18,... | collective-permute-start | bytes 4723208 | tf_op jit(solution)/shard_map/ppermute | solution.py:25
  1715.8 510.1 %collective-permute-start.14 = (f32[1,393600]{1,0:T(1,128)}, f32[1,393600]{1,0:T(1,128)}, u32[]{:S(2)}, u32[]{:S(2)}) collective-permute-start(f32[1,393600]{1,0:T(1,128)} %collective-permute-done.12), channel_id=1, source_target_pairs={{0,2},{2,4},{4,6},{6,8},{8,10},{10,12},{12,14},{14,16},{16,18},{18... | collective-permute-start | bytes 4723208 | tf_op jit(solution)/shard_map/ppermute | solution.py:22
  (110 other events, 1422.0 us)
Sparse Core Ops, SparseCore 0:
  9.6 299.1 all-gather.1
  770.7 721.7 all-reduce.2
